TPU v7x, 256 devices: a whole 4x4x8 slice. The times are simulated.
256 devices in a mesh: tile: 64 (over z, x, core), rot: 4 (over y).
Axes of the slice: x: 4, y: 4, z: 8, core: 2. Of those that a mesh axis runs over, the one named last changes fastest.
Arguments:
- tomogram: bfloat16 [2048, 5120], P('tile'), may hold values from -12 to 12
- templates: bfloat16 [16, 110592], P('rot', 'tile'), may hold values from -6 to 6
- valid: int32 [2048, 80], P('tile'), may hold values from 0 to 1, as said below
- quats: float32 [4, 4096], replicated, may hold values from -1 to 1, as said below
- rot_index: int32 [16], P('rot'), may hold values from 0 to 4095
Outputs:
- best: float32 [2048, 5120], P('tile', 'rot')
- evidence: float32 [2048, 5120], P('tile', 'rot')
- moments: float32 [4, 2048, 5120], P(None, 'tile', 'rot')
Inputs may be any that keep to these rules, and one draw needn't show every extreme that they name: `valid`: 1 marks a column (x, y) of voxels inside the lamella. `quats`: each column is a unit quaternion with a non-negative first component.
All inputs are finite; a program needn't handle non-finite values.
Results may differ from a plain program's by a relative error of at most 0.0003.
Values may be sent and summed in bfloat16 or wider, within the bound.
A program may use at most 128 MiB of HBM per device.

v0:
```python
import math
import jax
import jax.numpy as jnp
from jax import lax
from jax.sharding import PartitionSpec as P

TEMPL = 48
HALF = 24
EPSILON = 1e-06
TWO_PI = 2.0 * math.pi


def padded(block, sides, width):
    for axis, dim in sides:
        count = lax.axis_size(axis)
        forward = [(i, i + 1) for i in range(count - 1)]
        backward = [(target, source) for source, target in forward]
        low = lax.ppermute(
            lax.slice_in_dim(block, block.shape[dim] - width, None, axis=dim), axis, forward
        )
        high = lax.ppermute(lax.slice_in_dim(block, 0, width, axis=dim), axis, backward)
        block = jnp.concatenate([low, block, high], axis=dim)
    return block


def twiddle(count_in, shift_in, count_out, shift_out, length, direction, factor):
    row_idx = (jnp.arange(count_in, dtype=jnp.int32) + shift_in)[:, None]
    col_idx = (jnp.arange(count_out, dtype=jnp.int32) + shift_out)[None, :]
    phase_idx = jnp.remainder(row_idx * col_idx, length).astype(jnp.float32)
    angles = phase_idx * jnp.float32(direction * TWO_PI / length)
    real_part = jnp.cos(angles) * factor
    imag_part = jnp.sin(angles) * factor
    upper_half = jnp.stack([real_part, imag_part], axis=1)
    lower_half = jnp.stack([-imag_part, real_part], axis=1)
    return jnp.stack([upper_half, lower_half], axis=0)


def product(formula, left_arr, right_arr):
    return jnp.einsum(
        formula,
        left_arr,
        right_arr,
        precision=lax.Precision.HIGH,
        preferred_element_type=jnp.float32,
    )


def forward(volume, shift, direction, lengths):
    size_x, size_y, size_z = volume.shape
    table_z = twiddle(size_z, shift, lengths[2], 0, lengths[2], direction, 1.0)[0]
    spectrum = product("xyz,zdk->dxyk", volume, table_z)
    spectrum = product(
        "cxyz,cydk->dxkz",
        spectrum,
        twiddle(size_y, shift, lengths[1], 0, lengths[1], direction, 1.0),
    )
    return product(
        "cxyz,cxdk->dkyz",
        spectrum,
        twiddle(size_x, shift, lengths[0], 0, lengths[0], direction, 1.0),
    )


def inverse(spectrum, out_x, out_y, out_z, lengths):
    spectrum = product(
        "cxyz,cxdk->dkyz",
        spectrum,
        twiddle(lengths[0], 0, out_x, HALF, lengths[0], 1, 1.0 / lengths[0]),
    )
    spectrum = product(
        "cxyz,cydk->dxkz",
        spectrum,
        twiddle(lengths[1], 0, out_y, 0, lengths[1], 1, 1.0 / lengths[1]),
    )
    real_table = twiddle(lengths[2], 0, out_z, 0, lengths[2], 1, 1.0 / lengths[2])[:, :, 0]
    return product("cxyz,czk->xyk", spectrum, real_table)


def multiply(first_arr, other_arr):
    return jnp.stack(
        [
            first_arr[0] * other_arr[0] - first_arr[1] * other_arr[1],
            first_arr[0] * other_arr[1] + first_arr[1] * other_arr[0],
        ]
    )


def local(tomogram, templates, valid, quats, rot_index):
    x_cells, voxels = tomogram.shape
    y_cells = valid.shape[1]
    z_cells = voxels // y_cells
    lengths = (x_cells + TEMPL, y_cells + HALF, z_cells + HALF)
    widened = padded(tomogram, (("tile", 0),), HALF)
    slab_spectrum = forward(
        widened.astype(jnp.float32).reshape(x_cells + TEMPL, y_cells, z_cells), 0, -1, lengths
    )
    gathered_bank = lax.all_gather(templates, "tile", axis=1, tiled=True).astype(jnp.float32)
    centred = gathered_bank - jnp.mean(gathered_bank, axis=1, keepdims=True)
    tmpl_spread = jnp.sqrt(jnp.mean(centred * centred, axis=1, keepdims=True) + EPSILON)
    unit_bank = centred / (tmpl_spread * jnp.float32(TEMPL) ** 1.5)

    def correlate(unit_tmpl):
        tmpl_spectrum = forward(unit_tmpl.reshape(TEMPL, TEMPL, TEMPL), -HALF, 1, lengths)
        return inverse(multiply(slab_spectrum, tmpl_spectrum), x_cells, y_cells, z_cells, lengths)

    correlation = lax.map(correlate, unit_bank).reshape(unit_bank.shape[0], x_cells, voxels)
    inside = jnp.repeat(valid.astype(jnp.float32), z_cells, axis=1)
    columns = jnp.sum(valid.astype(jnp.float32))
    masked = correlation * inside[None]
    first_sum, all_columns = lax.psum((jnp.sum(masked, axis=(1, 2)), columns), "tile")
    voxel_count = all_columns * z_cells
    average = first_sum / voxel_count
    deviation = correlation - average[:, None, None]
    square_sum = lax.psum(jnp.sum(inside[None] * deviation * deviation, axis=(1, 2)), "tile")
    spread = jnp.sqrt(square_sum / voxel_count + EPSILON)
    scores = (correlation - average[:, None, None]) / spread[:, None, None]
    one_hot = (rot_index[:, None] == jnp.arange(quats.shape[1], dtype=jnp.int32)[None, :]).astype(
        jnp.float32
    )
    orient = product("rq,kq->rk", one_hot, quats)
    highest = jnp.max(scores, axis=0)
    weight = jnp.exp(scores - highest[None])
    exp_total = jnp.sum(weight, axis=0)
    moment = product("rxv,rk->kxv", weight, orient)
    groups = lax.axis_size("rot")
    share_len = voxels // groups
    offset = lax.axis_index("rot") * share_len
    high_full = lax.pmax(highest, "rot")
    rescale = jnp.exp(highest - high_full)
    total_full, moment_full = lax.psum((exp_total * rescale, moment * rescale[None]), "rot")
    high_all = lax.dynamic_slice_in_dim(high_full, offset, share_len, 1)
    total_all = lax.dynamic_slice_in_dim(total_full, offset, share_len, 1)
    moment_all = lax.dynamic_slice_in_dim(moment_full, offset, share_len, 2)
    inside_part = lax.dynamic_slice_in_dim(inside, offset, share_len, 1)
    best = inside_part * high_all
    evidence = inside_part * (high_all + jnp.log(total_all))
    moments = inside_part[None] * moment_all / total_all[None]
    return (best, evidence, moments)


def solution(mesh):
    placed = (P("tile", None), P("rot", "tile"), P("tile", None), P(), P("rot"))
    return jax.shard_map(
        local,
        mesh=mesh,
        in_specs=placed,
        out_specs=(P("tile", "rot"), P("tile", "rot"), P(None, "tile", "rot")),
        check_vma=False,
    )
```

profile of v0, /device:TPU:1, one launch (start us, length us, event | category | flops | bytes accessed | tf_op | source)
XLA Modules:
  0.0 683.0 jit_solution(3317119279552520776)
XLA Ops:
  7.2 1.8 fusion.124
  9.0 4.5 collective-permute-start
  13.5 1.9 collective-permute-start.1
  16.4 55.7 %all-gather = bf16[64,1728,4]{1,2,0:T(4,128)(2,1)S(1)} all-gather(bf16[1,1728,4]{1,2,0:T(4,128)(2,1)} %bitcast.196), channel_id=1, replica_groups=mesh['tile'=64,'rot'=4] {'tile'}, dimensions={0}, use_global_device_ids=true | all-gather | bytes 898560 | tf_op jit(solution)/shard_map/all_gather | solution.py:97
  74.6 2.8 reshape.771
  78.5 1.6 divide_bitcast_fusion
  82.6 1.5 reshape.767
  84.1 4.6 convolution_bitcast_fusion.1
  88.8 9.4 %copy.71 = f32[2,80,80,88,1]{2,1,0,4,3:T(8,128)} copy(f32[2,80,80,88,1]{3,2,1,0,4:T(8,128)} %convolution_bitcast_fusion.1) | data formatting | bytes 9011200 | tf_op jit(solution)/shard_map/xyz,zdk->dxyk/transpose | solution.py:39
  98.2 5.5 fusion.90
  103.7 5.6 fusion.83
  109.3 145.3 %while.13 = (s32[]{:T(128)}, f32[4,32,80,64]{2,3,1,0:T(8,128)}, f32[2,80,104,88]{2,1,3,0:T(8,128)}, f32[4,110592]{1,0:T(4,128)}, s32[]{:T(128)}) while((s32[]{:T(128)}, f32[4,32,80,64]{2,3,1,0:T(8,128)}, f32[2,80,104,88]{2,1,3,0:T(8,128)}, f32[4,110592]{1,0:T(4,128)}, s32[]{:T(128)}) %tuple.86), condition=%wide.region_3.4_spmd, body=%wide.region_2.3_spmd.sunk | while | flops 2770436608 | bytes 55842368 | solution.py:106
  109.6 2.8 dynamic-slice_reduce_fusion.2
  112.4 1.5 reshape.806
  114.1 2.3 convolution_bitcast_fusion.4
  116.4 4.6 copy.104
  121.0 3.8 fusion.158
  125.1 3.1 fusion.160
  128.1 5.9 multiply_subtract_fusion.2
  134.2 4.5 fusion.161
  139.1 3.5 fusion.163
  143.0 2.7 fusion.165
  145.9 2.8 dynamic-slice_reduce_fusion.2
  148.6 1.5 reshape.806
  150.3 2.3 convolution_bitcast_fusion.4
  152.7 4.6 copy.104
  157.2 3.8 fusion.158
  161.3 3.1 fusion.160
  164.4 5.9 multiply_subtract_fusion.2
  170.5 4.5 fusion.161
  175.4 3.5 fusion.163
  179.2 2.7 fusion.165
  182.1 2.8 dynamic-slice_reduce_fusion.2
  186.6 2.3 convolution_bitcast_fusion.4
  188.9 4.6 copy.104
  193.5 3.8 fusion.158
  197.5 3.1 fusion.160
  200.6 5.9 multiply_subtract_fusion.2
  206.7 4.5 fusion.161
  211.6 3.5 fusion.163
  215.4 2.7 fusion.165
  218.4 2.8 dynamic-slice_reduce_fusion.2
  222.8 2.3 convolution_bitcast_fusion.4
  225.1 4.6 copy.104
  229.7 3.8 fusion.158
  233.8 3.1 fusion.160
  236.8 5.9 multiply_subtract_fusion.2
  242.9 4.5 fusion.161
  247.8 3.5 fusion.163
  251.7 2.7 fusion.165
  254.6 2.8 multiply_reduce_fusion
  257.7 124.2 %all-reduce = (f32[4]{0:T(128)S(1)}, f32[]{:T(128)}) all-reduce(f32[4]{0:T(128)S(1)} %multiply_reduce_fusion, f32[]{:T(128)} %convert_reduce_fusion.1), channel_id=1, replica_groups=mesh['tile'=64,'rot'=4] {'tile'}, use_global_device_ids=true, to_apply=%region_5.6 | all-reduce | flops 5 | bytes 40 | tf_op jit(solution)/shard_map/psum | solution.py:110
  382.6 3.1 fusion.82
  385.7 5.7 copy.55
  391.4 126.6 %psum.37 = f32[4]{0:T(128)S(1)} all-reduce(f32[4]{0:T(128)S(1)} %fusion.82), channel_id=1, replica_groups=mesh['tile'=64,'rot'=4] {'tile'}, use_global_device_ids=true, to_apply=%region_9.10 | all-reduce | flops 4 | bytes 32 | tf_op jit(solution)/shard_map/psum | solution.py:114
  518.1 3.0 fusion.122
  521.5 4.4 exponential_reduce_fusion
  527.1 5.4 reshape.768
  534.2 2.2 subtract_exponential_fusion
  536.5 41.4 %all-reduce.5.cloned.1.call-done = f32[32,5120]{1,0:T(8,128)} async-done(((f32[32,5120]{1,0:T(8,128)}), f32[32,5120]{1,0:T(8,128)}) %all-reduce.5.cloned.1.call-update) | async-done | bytes 655376 | tf_op jit(solution)/shard_map/pmax | solution.py:128
  577.9 2.2 fusion.123
  580.1 5.6 convolution_multiply_fusion
  586.6 85.2 %all-reduce.7.cloned.1.call-done = (f32[32,5120]{1,0:T(8,128)}, f32[4,32,5120]{2,0,1:T(4,128)}) async-done(((f32[32,5120]{1,0:T(8,128)}, f32[4,32,5120]{2,0,1:T(4,128)}), (f32[32,5120]{1,0:T(8,128)}, f32[4,32,5120]{2,0,1:T(4,128)})) %all-reduce.7.cloned.1.call-update) | async-done | bytes 3276816 | tf_op jit(solution)/shard_map/psum | solution.py:130
  671.7 1.8 add_multiply_fusion
  (109 shorter events, 22.4 us)
Async XLA Ops:
  7.2 250.3 %copy-start = (f32[4,4096]{1,0:T(4,128)S(1)}, f32[4,4096]{1,0:T(4,128)}, u32[]{:S(2)}) copy-start(f32[4,4096]{1,0:T(4,128)} %param.10) | copy-start | bytes 196612
  7.2 570.7 %all-reduce.5.cloned.1.call-start = ((), (), s32[]{:S(2)}) async-start(), calls=%async_computation | async-start | bytes 1310720 | tf_op jit(solution)/shard_map/pmax | solution.py:128
  9.0 71.8 %collective-permute-start = (bf16[24,5120]{1,0:T(8,128)(2,1)}, bf16[24,5120]{1,0:T(8,128)(2,1)S(1)}, u32[]{:S(2)}, u32[]{:S(2)}) collective-permute-start(bf16[24,5120]{1,0:T(8,128)(2,1)} %get-tuple-element.138), channel_id=1, source_target_pairs={{0,4},{4,8},{8,12},{12,16},{16,20},{20,24},{24,28},{28,32},{32,36}... | collective-permute-start | bytes 737288 | tf_op jit(solution)/shard_map/ppermute | solution.py:18
  13.5 68.0 %collective-permute-start.1 = (bf16[24,5120]{1,0:T(8,128)(2,1)S(1)}, bf16[24,5120]{1,0:T(8,128)(2,1)}, u32[]{:S(2)}, u32[]{:S(2)}) collective-permute-start(bf16[24,5120]{1,0:T(8,128)(2,1)S(1)} %get-tuple-element.139), channel_id=1, source_target_pairs={{4,0},{8,4},{12,8},{16,12},{20,16},{24,20},{28,24},{32,28},{36,32}... | collective-permute-start | bytes 737288 | tf_op jit(solution)/shard_map/ppermute | solution.py:21
  74.6 5.6 copy-start.5
  77.4 4.1 copy-start.3
  80.8 0.7 copy-start.4
  254.6 2.9 copy-start.6
  527.1 5.4 copy-start.2
  532.5 1.7 copy-start.1
  534.2 137.5 %all-reduce.7.cloned.1.call-start = ((), (), s32[]{:S(2)}) async-start(), calls=%async_computation.1 | async-start | bytes 6553600 | tf_op jit(solution)/shard_map/psum | solution.py:130
Sparse Core Ops, SparseCore 0:
  534.3 43.5 all-reduce.4
  585.9 85.7 all-reduce.6
where the time goes:
time: 690 us; the launch traced here: 683 us
  blocking collectives  307 us (44%)
  waiting for transfers between devices  127 us (18%)
  matrix products  101 us (15%)
  local copies, waits for them, and re-layouts  69.1 us (10%)
  other arithmetic  56.8 us (8%)
  between operations  15.3 us (2%)
    psum x1, blocking collectives, local(): lax.psum(jnp.sum(inside[None] * deviation * deviation, axis=(1, 2)), 'tile')  127 us
    psum x1, blocking collectives, local(): lax.psum((jnp.sum(masked, axis=(1, 2)), columns), 'tile')  124 us
    dot_general x29, matrix products, product(): jnp.einsum(formula, left_arr, right_arr, precision=lax.Precision.HIGH, pr...  101 us
    psum x1, waiting for transfers between devices, local(): lax.psum((exp_total * rescale, moment * rescale[None]), 'rot')  85.2 us
    all_gather x1, blocking collectives, local(): lax.all_gather(templates, 'tile', axis=1, tiled=True).astype(jnp.float32)  55.7 us
    pmax x1, waiting for transfers between devices, local(): high_full = lax.pmax(highest, 'rot')  41.4 us
    transpose x5, local copies, waits for them, and re-layouts, product(): jnp.einsum(formula, left_arr, right_arr, precision=lax.Precision.HIGH, pr...  27.7 us
    sub x4, other arithmetic, multiply(): first_arr[0] * other_arr[0] - first_arr[1] * other_arr[1]  23.7 us
  transfers between devices with their start and end apart: 4, of which 2 were waited for; matrix products, arithmetic and copies ran while one was open for 2% of the time, Pallas kernels for 0%

commit v1 on v0

--- a/solution.py
+++ b/solution.py
@@ -94,7 +94,15 @@
     slab_spectrum = forward(
         widened.astype(jnp.float32).reshape(x_cells + TEMPL, y_cells, z_cells), 0, -1, lengths
     )
-    gathered_bank = lax.all_gather(templates, "tile", axis=1, tiled=True).astype(jnp.float32)
+
+    def draw_records(work_x, peer_axis="tile"):
+        found_now = lax.axis_size(peer_axis)
+        carry = jnp.stack([work_x] * found_now, 0)
+        base_arr = lax.all_to_all(carry, peer_axis, 0, 0)
+        small = jnp.concatenate(base_arr, 1)
+        return small
+
+    gathered_bank = draw_records(templates).astype(jnp.float32)
     centred = gathered_bank - jnp.mean(gathered_bank, axis=1, keepdims=True)
     tmpl_spread = jnp.sqrt(jnp.mean(centred * centred, axis=1, keepdims=True) + EPSILON)
     unit_bank = centred / (tmpl_spread * jnp.float32(TEMPL) ** 1.5)

time: 690 us -> 660 us (0.957)
  blocking collectives: 307 us -> 253 us
  starting transfers between devices: 6.52 us -> 19.5 us
  loops' own time: 0.79 us -> 12.2 us
  local copies, waits for them, and re-layouts: 69.1 us -> 62.1 us
    all_gather x1 -> x0, blocking collectives: 55.7 us -> none  [local(): lax.all_gather(templates, 'tile', axis=1, tiled=True).astype(jnp.float32)]
    all_to_all x0 -> x1, starting transfers between devices: none -> 13 us  [draw_records(): base_arr = lax.all_to_all(carry, peer_axis, 0, 0)]
    another operation x1, loops' own time: 0.79 us -> 12.2 us  [local(): lax.map(correlate, unit_bank).reshape(unit_bank.shape[0], x_cells, voxels)]
  transfers between devices with their start and end apart: 4 -> 5, of which waited for: 2 -> 2; matrix products, arithmetic and copies ran while one was open for 2% -> 5% of each run, Pallas kernels for 0% -> 0%
where the time goes in v1:
time: 660 us; the launch traced here: 649 us
  blocking collectives  253 us (38%)
  waiting for transfers between devices  126 us (19%)
  matrix products  102 us (15%)
  local copies, waits for them, and re-layouts  62.1 us (9%)
  other arithmetic  58.1 us (9%)
  starting transfers between devices  19.5 us (3%)
  between operations  15.3 us (2%)
  loops' own time  12.2 us (2%)
    psum x1, blocking collectives, local(): lax.psum(jnp.sum(inside[None] * deviation * deviation, axis=(1, 2)), 'tile')  129 us
    psum x1, blocking collectives, local(): lax.psum((jnp.sum(masked, axis=(1, 2)), columns), 'tile')  125 us
    dot_general x29, matrix products, product(): jnp.einsum(formula, left_arr, right_arr, precision=lax.Precision.HIGH, pr...  102 us
    psum x1, waiting for transfers between devices, local(): lax.psum((exp_total * rescale, moment * rescale[None]), 'rot')  85.2 us
    pmax x1, waiting for transfers between devices, local(): high_full = lax.pmax(highest, 'rot')  41.1 us
    transpose x5, local copies, waits for them, and re-layouts, product(): jnp.einsum(formula, left_arr, right_arr, precision=lax.Precision.HIGH, pr...  27.7 us
    sub x4, other arithmetic, multiply(): first_arr[0] * other_arr[0] - first_arr[1] * other_arr[1]  23.6 us
  transfers between devices with their start and end apart: 5, of which 2 were waited for; matrix products, arithmetic and copies ran while one was open for 5% of the time, Pallas kernels for 0%

profile of v1, /device:TPU:1, one launch (start us, length us, event | category | flops | bytes accessed | tf_op | source)
XLA Modules:
  0.0 649.0 jit_solution(17571526446893863086)
XLA Ops:
  8.4 4.5 collective-permute-start
  12.9 1.9 collective-permute-start.1
  14.8 1.9 stack.334
  16.7 13.0 %all-to-all-start = ((bf16[64,4,1728]{2,1,0:T(4,128)(2,1)}), bf16[64,4,1728]{2,1,0:T(4,128)(2,1)S(1)}, u32[]{:S(2)}, u32[]{:S(2)}) async-start(bf16[64,4,1728]{2,1,0:T(4,128)(2,1)} %stack.334), calls=%async_computation | async-start | bytes 1835008 | tf_op jit(solution)/shard_map/all_to_all | solution.py:101
  34.4 5.4 convolution_bitcast_fusion.1
  39.8 9.4 %copy.69 = f32[2,80,80,88,1]{2,1,0,4,3:T(8,128)} copy(f32[2,80,80,88,1]{3,2,1,0,4:T(8,128)} %convolution_bitcast_fusion.1) | data formatting | bytes 9011200 | tf_op jit(solution)/shard_map/xyz,zdk->dxyk/transpose | solution.py:39
  49.2 5.5 fusion.92
  54.8 5.6 fusion.83
  63.1 2.6 reshape.780
  65.7 1.8 subtract_divide_fusion.1
  67.6 150.8 %while.13 = (s32[]{:T(128)}, f32[4,32,80,64]{2,3,1,0:T(8,128)}, f32[2,80,104,88]{2,1,3,0:T(8,128)}, f32[4,110592]{1,0:T(4,128)S(1)}, s32[]{:T(128)}) while((s32[]{:T(128)}, f32[4,32,80,64]{2,3,1,0:T(8,128)}, f32[2,80,104,88]{2,1,3,0:T(8,128)}, f32[4,110592]{1,0:T(4,128)S(1)}, s32[]{:T(128)}) %tuple.86), condition=%wide.region_3.4_spmd, body=%wide.region_2.3_spmd.sunk | while | flops 2770436608 | bytes 69998200 | solution.py:114
  79.5 1.3 dynamic-slice_reduce_fusion.2
  80.7 1.5 reshape.815
  82.4 2.3 convolution_bitcast_fusion.4
  84.8 4.6 copy.102
  89.4 3.8 fusion.160
  93.4 3.1 fusion.162
  96.5 5.9 multiply_subtract_fusion.2
  102.6 4.5 fusion.163
  107.5 3.5 fusion.165
  111.3 2.7 fusion.167
  114.2 1.3 dynamic-slice_reduce_fusion.2
  115.5 1.5 reshape.815
  117.2 2.3 convolution_bitcast_fusion.4
  119.5 4.6 copy.102
  124.1 3.8 fusion.160
  128.2 3.1 fusion.162
  131.2 5.9 multiply_subtract_fusion.2
  137.3 4.5 fusion.163
  142.2 3.5 fusion.165
  146.1 2.7 fusion.167
  150.3 1.5 reshape.815
  152.0 2.3 convolution_bitcast_fusion.4
  154.3 4.6 copy.102
  158.9 3.8 fusion.160
  163.0 3.1 fusion.162
  166.0 5.9 multiply_subtract_fusion.2
  172.1 4.5 fusion.163
  177.0 3.5 fusion.165
  180.9 2.7 fusion.167
  185.1 1.5 reshape.815
  186.8 2.3 convolution_bitcast_fusion.4
  189.1 4.6 copy.102
  193.7 3.8 fusion.160
  197.8 3.1 fusion.162
  200.8 5.9 multiply_subtract_fusion.2
  206.9 4.5 fusion.163
  211.8 3.5 fusion.165
  215.7 2.7 fusion.167
  218.4 2.8 multiply_reduce_fusion
  221.5 124.6 %all-reduce = (f32[4]{0:T(128)S(1)}, f32[]{:T(128)}) all-reduce(f32[4]{0:T(128)S(1)} %multiply_reduce_fusion, f32[]{:T(128)} %convert_reduce_fusion.1), channel_id=1, replica_groups=mesh['tile'=64,'rot'=4] {'tile'}, use_global_device_ids=true, to_apply=%region_5.6 | all-reduce | flops 5 | bytes 40 | tf_op jit(solution)/shard_map/psum | solution.py:118
  346.8 3.1 fusion.82
  349.9 5.7 copy.53
  355.6 128.7 %psum.37 = f32[4]{0:T(128)S(1)} all-reduce(f32[4]{0:T(128)S(1)} %fusion.82), channel_id=1, replica_groups=mesh['tile'=64,'rot'=4] {'tile'}, use_global_device_ids=true, to_apply=%region_9.10 | all-reduce | flops 4 | bytes 32 | tf_op jit(solution)/shard_map/psum | solution.py:122
  484.3 3.0 fusion.124
  487.7 4.4 exponential_reduce_fusion
  493.4 5.4 reshape.779
  500.5 2.2 subtract_exponential_fusion
  502.8 41.1 %all-reduce.5.cloned.1.call-done = f32[32,5120]{1,0:T(8,128)} async-done(((f32[32,5120]{1,0:T(8,128)}), f32[32,5120]{1,0:T(8,128)}) %all-reduce.5.cloned.1.call-update) | async-done | bytes 655376 | tf_op jit(solution)/shard_map/pmax | solution.py:136
  543.9 2.2 fusion.125
  546.1 5.6 convolution_multiply_fusion
  552.6 85.2 %all-reduce.7.cloned.1.call-done = (f32[32,5120]{1,0:T(8,128)}, f32[4,32,5120]{2,0,1:T(4,128)}) async-done(((f32[32,5120]{1,0:T(8,128)}, f32[4,32,5120]{2,0,1:T(4,128)}), (f32[32,5120]{1,0:T(8,128)}, f32[4,32,5120]{2,0,1:T(4,128)})) %all-reduce.7.cloned.1.call-update) | async-done | bytes 3276816 | tf_op jit(solution)/shard_map/psum | solution.py:138
  637.7 1.8 add_multiply_fusion
  639.5 1.3 multiply_divide_fusion
  (132 shorter events, 22.2 us)
Async XLA Ops:
  7.2 214.1 %copy-start = (f32[4,4096]{1,0:T(4,128)S(1)}, f32[4,4096]{1,0:T(4,128)}, u32[]{:S(2)}) copy-start(f32[4,4096]{1,0:T(4,128)} %param.10) | copy-start | bytes 196612
  7.2 26.1 %copy-start.5 = (bf16[32,5120]{1,0:T(8,128)(2,1)S(1)}, bf16[32,5120]{1,0:T(8,128)(2,1)}, u32[]{:S(2)}) copy-start(bf16[32,5120]{1,0:T(8,128)(2,1)} %param.7) | copy-start | bytes 983044
  7.2 24.1 %copy-start.9 = (s32[32,80]{1,0:T(8,128)S(1)}, s32[32,80]{1,0:T(8,128)}, u32[]{:S(2)}) copy-start(s32[32,80]{1,0:T(8,128)} %param.9) | copy-start | bytes 30724
  8.4 24.9 %collective-permute-start = (bf16[24,5120]{1,0:T(8,128)(2,1)S(1)}, bf16[24,5120]{1,0:T(8,128)(2,1)S(1)}, u32[]{:S(2)}, u32[]{:S(2)}) collective-permute-start(bf16[24,5120]{1,0:T(8,128)(2,1)S(1)} %get-tuple-element.138), channel_id=1, source_target_pairs={{0,4},{4,8},{8,12},{12,16},{16,20},{20,24},{24,28},{28,32},{32,36}... | collective-permute-start | bytes 737288 | tf_op jit(solution)/shard_map/ppermute | solution.py:18
  12.9 20.4 %collective-permute-start.1 = (bf16[24,5120]{1,0:T(8,128)(2,1)S(1)}, bf16[24,5120]{1,0:T(8,128)(2,1)S(1)}, u32[]{:S(2)}, u32[]{:S(2)}) collective-permute-start(bf16[24,5120]{1,0:T(8,128)(2,1)S(1)} %get-tuple-element.139), channel_id=1, source_target_pairs={{4,0},{8,4},{12,8},{16,12},{20,16},{24,20},{28,24},{32,28},{36,32}... | collective-permute-start | bytes 737288 | tf_op jit(solution)/shard_map/ppermute | solution.py:21
  16.7 43.7 %all-to-all-start = ((bf16[64,4,1728]{2,1,0:T(4,128)(2,1)}), bf16[64,4,1728]{2,1,0:T(4,128)(2,1)S(1)}, u32[]{:S(2)}, u32[]{:S(2)}) async-start(bf16[64,4,1728]{2,1,0:T(4,128)(2,1)} %stack.334), calls=%async_computation | async-start | bytes 1835008 | tf_op jit(solution)/shard_map/all_to_all | solution.py:101
  29.7 514.2 %all-reduce.5.cloned.1.call-start = ((), (), s32[]{:S(2)}) async-start(), calls=%async_computation.1 | async-start | bytes 1310720 | tf_op jit(solution)/shard_map/pmax | solution.py:136
  39.8 9.4 %copy-start.6 = (f32[1,80,2,104]{3,1,0,2:T(8,128)S(1)}, f32[1,80,2,104]{3,1,0,2:T(8,128)}, u32[]{:S(2)}) copy-start(f32[1,80,2,104]{3,1,0,2:T(8,128)} %get-tuple-element.143) | copy-start | bytes 199684
  49.2 5.6 copy-start.7
  49.2 5.6 copy-start.8
  79.2 3.2 copy-start.2
  107.5 6.5 %copy-start.3 = (f32[4,110592]{1,0:T(4,128)S(1)}, f32[4,110592]{1,0:T(4,128)}, u32[]{:S(2)}) copy-start(f32[4,110592]{1,0:T(4,128)} %copy-done.2) | copy-start | bytes 5308420 | tf_op jit(solution)/shard_map/while
  114.0 3.2 copy-start.2
  142.2 6.6 %copy-start.3 = (f32[4,110592]{1,0:T(4,128)S(1)}, f32[4,110592]{1,0:T(4,128)}, u32[]{:S(2)}) copy-start(f32[4,110592]{1,0:T(4,128)} %copy-done.2) | copy-start | bytes 5308420 | tf_op jit(solution)/shard_map/while
  148.8 3.2 copy-start.2
  177.0 6.6 %copy-start.3 = (f32[4,110592]{1,0:T(4,128)S(1)}, f32[4,110592]{1,0:T(4,128)}, u32[]{:S(2)}) copy-start(f32[4,110592]{1,0:T(4,128)} %copy-done.2) | copy-start | bytes 5308420 | tf_op jit(solution)/shard_map/while
  183.6 3.2 copy-start.2
  211.8 6.6 %copy-start.3 = (f32[4,110592]{1,0:T(4,128)S(1)}, f32[4,110592]{1,0:T(4,128)}, u32[]{:S(2)}) copy-start(f32[4,110592]{1,0:T(4,128)} %copy-done.2) | copy-start | bytes 5308420 | tf_op jit(solution)/shard_map/while
  218.4 2.9 copy-start.10
  493.4 5.4 copy-start.4
  498.8 1.7 copy-start.1
  500.5 137.3 %all-reduce.7.cloned.1.call-start = ((), (), s32[]{:S(2)}) async-start(), calls=%async_computation.2 | async-start | bytes 6553600 | tf_op jit(solution)/shard_map/psum | solution.py:138
Sparse Core Ops, SparseCore 0:
  500.6 43.2 all-reduce.4
  551.9 85.7 all-reduce.6
